TPU v7x, 512 devices: a whole 4x8x8 slice. The times are simulated.
512 devices in a mesh: space: 64 (over y, z), orb: 8 (over x, core).
Axes of the slice: x: 4, y: 8, z: 8, core: 2. Of those that a mesh axis runs over, the one named last changes fastest.
Arguments:
- hamiltonian: bfloat16 [512, 7, 256, 256], P('space'), may hold values from -0.125 to 0.125
- orbitals: bfloat16 [256, 131072], P('orb', 'space'), may hold values from -6 to 6
- adjacency: int32 [512, 6], P('space'), may hold values from 0 to 511, as said below
Outputs:
- basis: float32 [256, 131072], P('orb', 'space')
- factor: float32 [256, 256], replicated
Inputs may be any that keep to these rules, and one draw needn't show every extreme that they name: `adjacency`: with elements in blocks of 8 (block b holds elements b * 8 to b * 8 + 7), face 0 of an element in block b lies in block b - 1 and face 1 in block b + 1 (both modulo the number of blocks), faces 2 to 5 in block b; for each face, the elements of a block name every element of the target block exactly once.
All inputs are finite; a program needn't handle non-finite values.
Results may differ from a plain program's by a relative error of at most 0.0041.
Values may be sent and summed in bfloat16 or wider, within the bound.
A program may use at most 64 MiB of HBM per device.

v0:
```python
import jax
import jax.numpy as jnp
from jax import lax
from jax.sharding import PartitionSpec as P

centre = 0.25
radius = 0.75


def with_halo(block, sides, width):
    for axis, dim in sides:
        count = lax.axis_size(axis)
        forward = [(i, i + 1) for i in range(count - 1)]
        forward.append((count - 1, 0))
        backward = [(target, source) for source, target in forward]
        low = lax.ppermute(
            lax.slice_in_dim(block, block.shape[dim] - width, None, axis=dim), axis, forward
        )
        high = lax.ppermute(lax.slice_in_dim(block, 0, width, axis=dim), axis, backward)
        block = jnp.concatenate([low, block, high], axis=dim)
    return block


def shards(hamiltonian, orbitals, adjacency):
    count = hamiltonian.shape[0]
    width = hamiltonian.shape[2]
    owned = orbitals.shape[0]
    total = count * lax.axis_size("space")
    first = lax.axis_index("space") * count
    located = (adjacency - first + count) % total

    def apply_ham(vec):
        padded = with_halo(vec, (("space", 1),), count * width)
        blocks = padded.reshape(owned, 3 * count, width)
        near = jnp.take(blocks, located.reshape(-1), axis=1).reshape(owned, count, 6, width)
        own_part = vec.reshape(owned, count, width)
        result = jnp.einsum(
            "oej,eij->oei", own_part, hamiltonian[:, 0], preferred_element_type=jnp.float32
        )
        result = result + jnp.einsum(
            "oefj,efij->oei", near, hamiltonian[:, 1:], preferred_element_type=jnp.float32
        )
        return result.reshape(owned, count * width)

    level_zero = orbitals.astype(jnp.float32)
    level_one = ((apply_ham(orbitals) - centre * level_zero) / radius).astype(jnp.bfloat16)
    one_wide = level_one.astype(jnp.float32)
    level_two = (2.0 * (apply_ham(level_one) - centre * one_wide) / radius - level_zero).astype(
        jnp.bfloat16
    )
    two_wide = level_two.astype(jnp.float32)
    filtered = 2.0 * (apply_ham(level_two) - centre * two_wide) / radius - one_wide
    row_piece = lax.all_to_all(filtered, "orb", split_axis=1, concat_axis=0, tiled=True)
    partial_gram = jnp.dot(row_piece, row_piece.T, precision=lax.Precision.HIGHEST)
    gram = lax.psum(partial_gram, ("space", "orb"))
    lower = jnp.linalg.cholesky(gram)
    solved = lax.linalg.triangular_solve(lower, row_piece, left_side=True, lower=True)
    basis = lax.all_to_all(solved, "orb", split_axis=0, concat_axis=1, tiled=True)
    return (basis, lower.T)


def solution(mesh):
    in_specs = (P("space", None, None, None), P("orb", "space"), P("space", None))
    out_specs = (P("orb", "space"), P())
    return jax.shard_map(shards, mesh=mesh, in_specs=in_specs, out_specs=out_specs, check_vma=False)
```

profile of v0, /device:TPU:24, one launch (start us, length us, event | category | flops | bytes accessed | tf_op | source)
XLA Modules:
  0.0 435.6 jit_solution(6208198198700955853)
XLA Ops:
  7.2 4.4 %collective-permute-start = (bf16[32,2048]{1,0:T(8,128)(2,1)}, bf16[32,2048]{1,0:T(8,128)(2,1)S(1)}, u32[]{:S(2)}, u32[]{:S(2)}) collective-permute-start(bf16[32,2048]{1,0:T(8,128)(2,1)} %param.6), channel_id=1, source_target_pairs={{0,8},{8,16},{16,24},{24,32},{32,40},{40,48},{48,56},{56,64},{64,7... | collective-permute-start | bytes 393224 | tf_op jit(solution)/shard_map/ppermute | solution.py:16
  11.6 8.5 %collective-permute-start.1 = (bf16[32,2048]{1,0:T(8,128)(2,1)}, bf16[32,2048]{1,0:T(8,128)(2,1)S(1)}, u32[]{:S(2)}, u32[]{:S(2)}) collective-permute-start(bf16[32,2048]{1,0:T(8,128)(2,1)} %param.6), channel_id=1, source_target_pairs={{8,0},{16,8},{24,16},{32,24},{40,32},{48,40},{56,48},{64,56},{72,6... | collective-permute-start | bytes 393224 | tf_op jit(solution)/shard_map/ppermute | solution.py:19
  24.9 4.7 %fusion.6 = f32[32,8,256]{2,0,1:T(8,128)S(1)} fusion(bf16[32,8,6,256]{3,0,2,1:T(8,128)(2,1)S(1)} %bitcast.139, bf16[8,7,256,256]{3,2,1,0:T(8,128)(2,1)} %param.5), kind=kOutput, calls=%fused_computation.11 | convolution fusion | flops 201326592 | bytes 7340032 | tf_op jit(solution)/shard_map/oefj,efij->oei/dot_general | solution.py:40
  29.6 1.6 fusion.16
  31.3 1.9 collective-permute-start.2
  33.3 6.4 %collective-permute-start.3 = (bf16[32,2048]{1,0:T(8,128)(2,1)S(1)}, bf16[32,2048]{1,0:T(8,128)(2,1)S(1)}, u32[]{:S(2)}, u32[]{:S(2)}) collective-permute-start(bf16[32,2048]{1,0:T(8,128)(2,1)S(1)} %fusion.27), channel_id=1, source_target_pairs={{8,0},{16,8},{24,16},{32,24},{40,32},{48,40},{56,48},{64,56},{72,6... | collective-permute-start | bytes 393224 | tf_op jit(solution)/shard_map/ppermute | solution.py:19
  40.7 1.5 collective-permute-done.3
  43.0 4.7 %fusion.9 = f32[8,32,256]{2,1,0:T(8,128)S(1)} fusion(bf16[32,8,6,256]{3,0,2,1:T(8,128)(2,1)S(1)} %bitcast.140, bf16[8,7,256,256]{3,2,1,0:T(8,128)(2,1)} %param.5), kind=kOutput, calls=%fused_computation.12 | convolution fusion | flops 201326592 | bytes 7340032 | tf_op jit(solution)/shard_map/oefj,efij->oei/dot_general | solution.py:40
  47.7 1.7 fusion.18
  49.5 2.9 collective-permute-start.4
  52.4 5.5 %collective-permute-start.5 = (bf16[32,2048]{1,0:T(8,128)(2,1)S(1)}, bf16[32,2048]{1,0:T(8,128)(2,1)S(1)}, u32[]{:S(2)}, u32[]{:S(2)}) collective-permute-start(bf16[32,2048]{1,0:T(8,128)(2,1)S(1)} %fusion.28), channel_id=1, source_target_pairs={{8,0},{16,8},{24,16},{32,24},{40,32},{48,40},{56,48},{64,56},{72,6... | collective-permute-start | bytes 393224 | tf_op jit(solution)/shard_map/ppermute | solution.py:19
  58.9 1.5 collective-permute-done.5
  61.2 4.7 %fusion.12 = f32[8,32,256]{2,1,0:T(8,128)S(1)} fusion(bf16[32,8,6,256]{3,0,2,1:T(8,128)(2,1)S(1)} %bitcast.138, bf16[8,7,256,256]{3,2,1,0:T(8,128)(2,1)} %param.5), kind=kOutput, calls=%fused_computation.13 | convolution fusion | flops 201326592 | bytes 7340032 | tf_op jit(solution)/shard_map/oefj,efij->oei/dot_general | solution.py:40
  65.9 1.7 fusion.17
  68.4 4.3 all-to-all-start
  73.0 7.3 %all-to-all-done = f32[32,8,256]{2,0,1:T(8,128)S(1)} async-done(((f32[32,8,256]{2,0,1:T(8,128)}), f32[32,8,256]{2,0,1:T(8,128)S(1)}, u32[]{:S(2)}, u32[]{:S(2)}) %all-to-all-start) | async-done | bytes 262176 | tf_op jit(solution)/shard_map/all_to_all | solution.py:53
  81.4 271.7 %all-reduce.3.cloned.1.call-done = f32[256,256]{0,1:T(8,128)} async-done(((f32[256,256]{0,1:T(8,128)}), f32[256,256]{0,1:T(8,128)}) %all-reduce.3.cloned.1.call-update) | async-done | bytes 262160 | tf_op jit(solution)/shard_map/psum | solution.py:55
  355.2 11.7 %cholesky.50 = f32[128,128]{1,0:T(8,128)S(1)} custom-call(f32[128,128]{1,0:T(8,128)S(1)} %cholesky.118), custom_call_target="Cholesky" | custom-call | tf_op jit(solution)/shard_map/jit(cholesky)/cholesky | solution.py:56
  366.9 9.8 %custom-call.14 = f32[1,128,128]{1,2,0:T(8,128)S(1)} custom-call(f32[1,128,128]{2,1,0:T(8,128)S(1)} %get-tuple-element.34), custom_call_target="InvertDiagBlocksLowerTriangular" | custom-call | tf_op jit(solution)/shard_map/jit(cholesky)/cholesky | solution.py:56
  377.2 11.7 %cholesky.105 = f32[128,128]{1,0:T(8,128)S(1)} custom-call(f32[128,128]{1,0:T(8,128)S(1)} %convolution_subtract_fusion.1), custom_call_target="Cholesky" | custom-call | tf_op jit(solution)/shard_map/jit(cholesky)/cholesky | solution.py:56
  391.0 4.0 while.1
  395.0 19.7 %custom-call.15 = f32[2,128,128]{1,2,0:T(8,128)S(1)} custom-call(f32[2,128,128]{2,1,0:T(8,128)S(1)} %get-tuple-element.10), custom_call_target="InvertDiagBlocksLowerTriangular" | custom-call | tf_op jit(solution)/shard_map/triangular_solve | solution.py:57
  416.3 4.3 all-to-all-start.1
  421.4 6.7 %all-to-all-done.1 = f32[8,32,256]{2,1,0:T(8,128)S(1)} async-done(((f32[8,32,256]{2,1,0:T(8,128)}), f32[8,32,256]{2,1,0:T(8,128)S(1)}, u32[]{:S(2)}, u32[]{:S(2)}) %all-to-all-start.1) | async-done | bytes 262176 | tf_op jit(solution)/shard_map/all_to_all | solution.py:58
  (59 shorter events, 21.1 us)
Async XLA Ops:
  7.2 22.4 %copy-start = (bf16[32,2048]{1,0:T(8,128)(2,1)S(1)}, bf16[32,2048]{1,0:T(8,128)(2,1)}, u32[]{:S(2)}) copy-start(bf16[32,2048]{1,0:T(8,128)(2,1)} %param.6) | copy-start | bytes 393220
  7.2 14.7 %collective-permute-start = (bf16[32,2048]{1,0:T(8,128)(2,1)}, bf16[32,2048]{1,0:T(8,128)(2,1)S(1)}, u32[]{:S(2)}, u32[]{:S(2)}) collective-permute-start(bf16[32,2048]{1,0:T(8,128)(2,1)} %param.6), channel_id=1, source_target_pairs={{0,8},{8,16},{16,24},{24,32},{32,40},{40,48},{48,56},{56,64},{64,7... | collective-permute-start | bytes 393224 | tf_op jit(solution)/shard_map/ppermute | solution.py:16
  11.6 11.5 %collective-permute-start.1 = (bf16[32,2048]{1,0:T(8,128)(2,1)}, bf16[32,2048]{1,0:T(8,128)(2,1)S(1)}, u32[]{:S(2)}, u32[]{:S(2)}) collective-permute-start(bf16[32,2048]{1,0:T(8,128)(2,1)} %param.6), channel_id=1, source_target_pairs={{8,0},{16,8},{24,16},{32,24},{40,32},{48,40},{56,48},{64,56},{72,6... | collective-permute-start | bytes 393224 | tf_op jit(solution)/shard_map/ppermute | solution.py:19
  31.3 9.3 %collective-permute-start.2 = (bf16[32,2048]{1,0:T(8,128)(2,1)S(1)}, bf16[32,2048]{1,0:T(8,128)(2,1)S(1)}, u32[]{:S(2)}, u32[]{:S(2)}) collective-permute-start(bf16[32,2048]{1,0:T(8,128)(2,1)S(1)} %fusion.27), channel_id=1, source_target_pairs={{0,8},{8,16},{16,24},{24,32},{32,40},{40,48},{48,56},{56,64},{64,7... | collective-permute-start | bytes 393224 | tf_op jit(solution)/shard_map/ppermute | solution.py:16
  33.3 8.9 %collective-permute-start.3 = (bf16[32,2048]{1,0:T(8,128)(2,1)S(1)}, bf16[32,2048]{1,0:T(8,128)(2,1)S(1)}, u32[]{:S(2)}, u32[]{:S(2)}) collective-permute-start(bf16[32,2048]{1,0:T(8,128)(2,1)S(1)} %fusion.27), channel_id=1, source_target_pairs={{8,0},{16,8},{24,16},{32,24},{40,32},{48,40},{56,48},{64,56},{72,6... | collective-permute-start | bytes 393224 | tf_op jit(solution)/shard_map/ppermute | solution.py:19
  49.5 9.4 %collective-permute-start.4 = (bf16[32,2048]{1,0:T(8,128)(2,1)S(1)}, bf16[32,2048]{1,0:T(8,128)(2,1)S(1)}, u32[]{:S(2)}, u32[]{:S(2)}) collective-permute-start(bf16[32,2048]{1,0:T(8,128)(2,1)S(1)} %fusion.28), channel_id=1, source_target_pairs={{0,8},{8,16},{16,24},{24,32},{32,40},{40,48},{48,56},{56,64},{64,7... | collective-permute-start | bytes 393224 | tf_op jit(solution)/shard_map/ppermute | solution.py:16
  52.4 8.0 %collective-permute-start.5 = (bf16[32,2048]{1,0:T(8,128)(2,1)S(1)}, bf16[32,2048]{1,0:T(8,128)(2,1)S(1)}, u32[]{:S(2)}, u32[]{:S(2)}) collective-permute-start(bf16[32,2048]{1,0:T(8,128)(2,1)S(1)} %fusion.28), channel_id=1, source_target_pairs={{8,0},{16,8},{24,16},{32,24},{40,32},{48,40},{56,48},{64,56},{72,6... | collective-permute-start | bytes 393224 | tf_op jit(solution)/shard_map/ppermute | solution.py:19
  68.4 11.8 %all-to-all-start = ((f32[32,8,256]{2,0,1:T(8,128)}), f32[32,8,256]{2,0,1:T(8,128)S(1)}, u32[]{:S(2)}, u32[]{:S(2)}) async-start(f32[32,8,256]{2,0,1:T(8,128)} %bitcast.115), calls=%async_computation | async-start | bytes 524288 | tf_op jit(solution)/shard_map/all_to_all | solution.py:53
  72.7 280.4 %all-reduce.3.cloned.1.call-start = ((), (), s32[]{:S(2)}) async-start(), calls=%async_computation.2 | async-start | bytes 524288 | tf_op jit(solution)/shard_map/psum | solution.py:55
  416.3 11.8 %all-to-all-start.1 = ((f32[8,32,256]{2,1,0:T(8,128)}), f32[8,32,256]{2,1,0:T(8,128)S(1)}, u32[]{:S(2)}, u32[]{:S(2)}) async-start(f32[8,32,256]{2,1,0:T(8,128)} %bitcast.26), calls=%async_computation.1 | async-start | bytes 524288 | tf_op jit(solution)/shard_map/all_to_all | solution.py:58
Sparse Core Ops, SparseCore 0:
  81.5 271.5 all-reduce.2
where the time goes:
time: 436 us
  waiting for transfers between devices  293 us (67%)
  other arithmetic  57.7 us (13%)
  starting transfers between devices  38.4 us (9%)
  matrix products  21.5 us (5%)
  between operations  15.6 us (4%)
  local copies, waits for them, and re-layouts  9.42 us (2%)
    psum x1, waiting for transfers between devices, shards(): gram = lax.psum(partial_gram, ('space', 'orb'))  272 us
    another operation x6, other arithmetic, shards(): lower = jnp.linalg.cholesky(gram)  33.9 us
    another operation x3, other arithmetic, shards(): lax.linalg.triangular_solve(lower, row_piece, left_side=True, lower=True)  20.4 us
    ppermute x3, starting transfers between devices, with_halo(): lax.ppermute(lax.slice_in_dim(block, 0, width, axis=dim), axis, backward)  20.3 us
    dot_general x3, matrix products, apply_ham(): jnp.einsum('oefj,efij->oei', near, hamiltonian[:, 1:], preferred_element_...  14.1 us
    ppermute x3, starting transfers between devices, with_halo(): lax.ppermute(lax.slice_in_dim(block, block.shape[dim] - width, None, axis...  9.26 us
  transfers between devices with their start and end apart: 9, of which 9 were waited for; matrix products, arithmetic and copies ran while one was open for 0% of the time, Pallas kernels for 0%

commit v1 on v0

--- a/solution.py
+++ b/solution.py
@@ -52,7 +52,8 @@
     filtered = 2.0 * (apply_ham(level_two) - centre * two_wide) / radius - one_wide
     row_piece = lax.all_to_all(filtered, "orb", split_axis=1, concat_axis=0, tiled=True)
     partial_gram = jnp.dot(row_piece, row_piece.T, precision=lax.Precision.HIGHEST)
-    gram = lax.psum(partial_gram, ("space", "orb"))
+    local_part = lax.psum(partial_gram, "orb")
+    gram = lax.psum(local_part, "space")
     lower = jnp.linalg.cholesky(gram)
     solved = lax.linalg.triangular_solve(lower, row_piece, left_side=True, lower=True)
     basis = lax.all_to_all(solved, "orb", split_axis=0, concat_axis=1, tiled=True)

time: 436 us -> 391 us (0.90)
  the two profiles are of different devices: /device:TPU:24 before, /device:TPU:1 now
where the time goes in v1:
time: 391 us; the launch traced here: 390 us
  waiting for transfers between devices  229 us (59%)
  other arithmetic  57.7 us (15%)
  starting transfers between devices  44.1 us (11%)
  matrix products  21.5 us (5%)
  between operations  15.6 us (4%)
  blocking collectives  14.1 us (4%)
  local copies, waits for them, and re-layouts  8.71 us (2%)
    psum x1, waiting for transfers between devices, shards(): gram = lax.psum(local_part, 'space')  153 us
    psum x1, waiting for transfers between devices, shards(): local_part = lax.psum(partial_gram, 'orb')  64.3 us
    another operation x6, other arithmetic, shards(): lower = jnp.linalg.cholesky(gram)  33.9 us
    ppermute x3, starting transfers between devices, with_halo(): lax.ppermute(lax.slice_in_dim(block, 0, width, axis=dim), axis, backward)  25.9 us
    another operation x3, other arithmetic, shards(): lax.linalg.triangular_solve(lower, row_piece, left_side=True, lower=True)  20.4 us
    dot_general x3, matrix products, apply_ham(): jnp.einsum('oefj,efij->oei', near, hamiltonian[:, 1:], preferred_element_...  14.1 us
    all_to_all x1, blocking collectives, shards(): lax.all_to_all(filtered, 'orb', split_axis=1, concat_axis=0, tiled=True)  14.1 us
    all_to_all x1, starting transfers between devices, shards(): lax.all_to_all(solved, 'orb', split_axis=0, concat_axis=1, tiled=True)  9.28 us
  transfers between devices with their start and end apart: 9, of which 9 were waited for; matrix products, arithmetic and copies ran while one was open for 0% of the time, Pallas kernels for 0%

profile of v1, /device:TPU:1, one launch (start us, length us, event | category | flops | bytes accessed | tf_op | source)
XLA Modules:
  0.0 390.5 jit_solution(15790222764679077060)
XLA Ops:
  7.2 4.8 %collective-permute-start = (bf16[32,2048]{1,0:T(8,128)(2,1)}, bf16[32,2048]{1,0:T(8,128)(2,1)S(1)}, u32[]{:S(2)}, u32[]{:S(2)}) collective-permute-start(bf16[32,2048]{1,0:T(8,128)(2,1)} %param.6), channel_id=1, source_target_pairs={{0,8},{8,16},{16,24},{24,32},{32,40},{40,48},{48,56},{56,64},{64,7... | collective-permute-start | bytes 393224 | tf_op jit(solution)/shard_map/ppermute | solution.py:16
  12.0 11.5 %collective-permute-start.1 = (bf16[32,2048]{1,0:T(8,128)(2,1)}, bf16[32,2048]{1,0:T(8,128)(2,1)S(1)}, u32[]{:S(2)}, u32[]{:S(2)}) collective-permute-start(bf16[32,2048]{1,0:T(8,128)(2,1)} %param.6), channel_id=1, source_target_pairs={{8,0},{16,8},{24,16},{32,24},{40,32},{48,40},{56,48},{64,56},{72,6... | collective-permute-start | bytes 393224 | tf_op jit(solution)/shard_map/ppermute | solution.py:19
  27.8 4.7 %fusion.6 = f32[32,8,256]{2,0,1:T(8,128)S(1)} fusion(bf16[32,8,6,256]{3,0,2,1:T(8,128)(2,1)S(1)} %bitcast.140, bf16[8,7,256,256]{3,2,1,0:T(8,128)(2,1)} %param.5), kind=kOutput, calls=%fused_computation.11 | convolution fusion | flops 201326592 | bytes 7340032 | tf_op jit(solution)/shard_map/oefj,efij->oei/dot_general | solution.py:40
  32.5 1.6 fusion.16
  34.2 1.9 collective-permute-start.2
  36.2 7.3 %collective-permute-start.3 = (bf16[32,2048]{1,0:T(8,128)(2,1)S(1)}, bf16[32,2048]{1,0:T(8,128)(2,1)S(1)}, u32[]{:S(2)}, u32[]{:S(2)}) collective-permute-start(bf16[32,2048]{1,0:T(8,128)(2,1)S(1)} %fusion.27), channel_id=1, source_target_pairs={{8,0},{16,8},{24,16},{32,24},{40,32},{48,40},{56,48},{64,56},{72,6... | collective-permute-start | bytes 393224 | tf_op jit(solution)/shard_map/ppermute | solution.py:19
  43.9 1.5 collective-permute-done.3
  46.3 4.7 %fusion.9 = f32[8,32,256]{2,1,0:T(8,128)S(1)} fusion(bf16[32,8,6,256]{3,0,2,1:T(8,128)(2,1)S(1)} %bitcast.141, bf16[8,7,256,256]{3,2,1,0:T(8,128)(2,1)} %param.5), kind=kOutput, calls=%fused_computation.12 | convolution fusion | flops 201326592 | bytes 7340032 | tf_op jit(solution)/shard_map/oefj,efij->oei/dot_general | solution.py:40
  51.0 1.7 fusion.18
  52.7 1.9 collective-permute-start.4
  54.7 7.1 %collective-permute-start.5 = (bf16[32,2048]{1,0:T(8,128)(2,1)S(1)}, bf16[32,2048]{1,0:T(8,128)(2,1)S(1)}, u32[]{:S(2)}, u32[]{:S(2)}) collective-permute-start(bf16[32,2048]{1,0:T(8,128)(2,1)S(1)} %fusion.28), channel_id=1, source_target_pairs={{8,0},{16,8},{24,16},{32,24},{40,32},{48,40},{56,48},{64,56},{72,6... | collective-permute-start | bytes 393224 | tf_op jit(solution)/shard_map/ppermute | solution.py:19
  62.2 1.5 collective-permute-done.5
  64.6 4.7 %fusion.12 = f32[8,32,256]{2,1,0:T(8,128)S(1)} fusion(bf16[32,8,6,256]{3,0,2,1:T(8,128)(2,1)S(1)} %bitcast.139, bf16[8,7,256,256]{3,2,1,0:T(8,128)(2,1)} %param.5), kind=kOutput, calls=%fused_computation.13 | convolution fusion | flops 201326592 | bytes 7340032 | tf_op jit(solution)/shard_map/oefj,efij->oei/dot_general | solution.py:40
  69.3 1.7 fusion.17
  71.0 14.1 %all_to_all.38 = f32[32,8,256]{2,0,1:T(8,128)S(1)} all-to-all(f32[32,8,256]{2,0,1:T(8,128)S(1)} %bitcast.138), channel_id=1, replica_groups=mesh['space'=64,'orb'=8] {'orb'}, dimensions={1} | all-to-all | bytes 524288 | tf_op jit(solution)/shard_map/all_to_all | solution.py:53
  86.5 64.3 %all-reduce.4.cloned.1.call-done = f32[256,256]{0,1:T(8,128)} async-done(((f32[256,256]{0,1:T(8,128)}), f32[256,256]{0,1:T(8,128)}) %all-reduce.4.cloned.1.call-update) | async-done | bytes 262160 | tf_op jit(solution)/shard_map/psum | solution.py:55
  150.9 153.1 %all-reduce.6.cloned.1.call-done = f32[256,256]{0,1:T(8,128)} async-done(((f32[256,256]{0,1:T(8,128)}), f32[256,256]{0,1:T(8,128)}) %all-reduce.6.cloned.1.call-update) | async-done | bytes 262160 | tf_op jit(solution)/shard_map/psum | solution.py:56
  306.1 11.7 %cholesky.50 = f32[128,128]{1,0:T(8,128)S(1)} custom-call(f32[128,128]{1,0:T(8,128)S(1)} %cholesky.118), custom_call_target="Cholesky" | custom-call | tf_op jit(solution)/shard_map/jit(cholesky)/cholesky | solution.py:57
  317.8 9.8 %custom-call.14 = f32[1,128,128]{1,2,0:T(8,128)S(1)} custom-call(f32[1,128,128]{2,1,0:T(8,128)S(1)} %get-tuple-element.34), custom_call_target="InvertDiagBlocksLowerTriangular" | custom-call | tf_op jit(solution)/shard_map/jit(cholesky)/cholesky | solution.py:57
  328.1 11.7 %cholesky.105 = f32[128,128]{1,0:T(8,128)S(1)} custom-call(f32[128,128]{1,0:T(8,128)S(1)} %convolution_subtract_fusion.1), custom_call_target="Cholesky" | custom-call | tf_op jit(solution)/shard_map/jit(cholesky)/cholesky | solution.py:57
  341.8 4.0 %while.1 = (s32[]{:T(128)}, f32[256,256]{1,0:T(8,128)S(1)}, s32[2,2]{1,0:T(2,128)S(1)}, f32[2,128,128]{2,1,0:T(8,128)S(1)}, s32[]{:T(128)}) while((s32[]{:T(128)}, f32[256,256]{1,0:T(8,128)S(1)}, s32[2,2]{1,0:T(2,128)S(1)}, f32[2,128,128]{2,1,0:T(8,128)S(1)}, s32[]{:T(128)}) %tuple.33), condition=%wide.while_cond, body=%wide.while_body.sunk | while | flops 2 | bytes 131181 | solution.py:58
  345.8 19.7 %custom-call.15 = f32[2,128,128]{1,2,0:T(8,128)S(1)} custom-call(f32[2,128,128]{2,1,0:T(8,128)S(1)} %get-tuple-element.10), custom_call_target="InvertDiagBlocksLowerTriangular" | custom-call | tf_op jit(solution)/shard_map/triangular_solve | solution.py:58
  367.1 9.3 %all-to-all-start.1 = ((f32[8,32,256]{2,1,0:T(8,128)}), f32[8,32,256]{2,1,0:T(8,128)S(1)}, u32[]{:S(2)}, u32[]{:S(2)}) async-start(f32[8,32,256]{2,1,0:T(8,128)} %bitcast.26), calls=%async_computation.1 | async-start | bytes 524288 | tf_op jit(solution)/shard_map/all_to_all | solution.py:59
  377.3 5.6 %all-to-all-done.1 = f32[8,32,256]{2,1,0:T(8,128)S(1)} async-done(((f32[8,32,256]{2,1,0:T(8,128)}), f32[8,32,256]{2,1,0:T(8,128)S(1)}, u32[]{:S(2)}, u32[]{:S(2)}) %all-to-all-start.1) | async-done | bytes 262176 | tf_op jit(solution)/shard_map/all_to_all | solution.py:59
  (61 shorter events, 18.7 us)
Async XLA Ops:
  7.2 25.3 %copy-start = (bf16[32,2048]{1,0:T(8,128)(2,1)S(1)}, bf16[32,2048]{1,0:T(8,128)(2,1)}, u32[]{:S(2)}) copy-start(bf16[32,2048]{1,0:T(8,128)(2,1)} %param.6) | copy-start | bytes 393220
  7.2 143.6 %all-reduce.4.cloned.1.call-start = ((), (), s32[]{:S(2)}) async-start(), calls=%async_computation.2 | async-start | bytes 524288 | tf_op jit(solution)/shard_map/psum | solution.py:55
  7.2 17.8 %collective-permute-start = (bf16[32,2048]{1,0:T(8,128)(2,1)}, bf16[32,2048]{1,0:T(8,128)(2,1)S(1)}, u32[]{:S(2)}, u32[]{:S(2)}) collective-permute-start(bf16[32,2048]{1,0:T(8,128)(2,1)} %param.6), channel_id=1, source_target_pairs={{0,8},{8,16},{16,24},{24,32},{32,40},{40,48},{48,56},{56,64},{64,7... | collective-permute-start | bytes 393224 | tf_op jit(solution)/shard_map/ppermute | solution.py:16
  12.0 14.0 %collective-permute-start.1 = (bf16[32,2048]{1,0:T(8,128)(2,1)}, bf16[32,2048]{1,0:T(8,128)(2,1)S(1)}, u32[]{:S(2)}, u32[]{:S(2)}) collective-permute-start(bf16[32,2048]{1,0:T(8,128)(2,1)} %param.6), channel_id=1, source_target_pairs={{8,0},{16,8},{24,16},{32,24},{40,32},{48,40},{56,48},{64,56},{72,6... | collective-permute-start | bytes 393224 | tf_op jit(solution)/shard_map/ppermute | solution.py:19
  34.2 9.7 %collective-permute-start.2 = (bf16[32,2048]{1,0:T(8,128)(2,1)S(1)}, bf16[32,2048]{1,0:T(8,128)(2,1)S(1)}, u32[]{:S(2)}, u32[]{:S(2)}) collective-permute-start(bf16[32,2048]{1,0:T(8,128)(2,1)S(1)} %fusion.27), channel_id=1, source_target_pairs={{0,8},{8,16},{16,24},{24,32},{32,40},{40,48},{48,56},{56,64},{64,7... | collective-permute-start | bytes 393224 | tf_op jit(solution)/shard_map/ppermute | solution.py:16
  36.2 9.3 %collective-permute-start.3 = (bf16[32,2048]{1,0:T(8,128)(2,1)S(1)}, bf16[32,2048]{1,0:T(8,128)(2,1)S(1)}, u32[]{:S(2)}, u32[]{:S(2)}) collective-permute-start(bf16[32,2048]{1,0:T(8,128)(2,1)S(1)} %fusion.27), channel_id=1, source_target_pairs={{8,0},{16,8},{24,16},{32,24},{40,32},{48,40},{56,48},{64,56},{72,6... | collective-permute-start | bytes 393224 | tf_op jit(solution)/shard_map/ppermute | solution.py:19
  52.7 9.4 %collective-permute-start.4 = (bf16[32,2048]{1,0:T(8,128)(2,1)S(1)}, bf16[32,2048]{1,0:T(8,128)(2,1)S(1)}, u32[]{:S(2)}, u32[]{:S(2)}) collective-permute-start(bf16[32,2048]{1,0:T(8,128)(2,1)S(1)} %fusion.28), channel_id=1, source_target_pairs={{0,8},{8,16},{16,24},{24,32},{32,40},{40,48},{48,56},{56,64},{64,7... | collective-permute-start | bytes 393224 | tf_op jit(solution)/shard_map/ppermute | solution.py:16
  54.7 9.0 %collective-permute-start.5 = (bf16[32,2048]{1,0:T(8,128)(2,1)S(1)}, bf16[32,2048]{1,0:T(8,128)(2,1)S(1)}, u32[]{:S(2)}, u32[]{:S(2)}) collective-permute-start(bf16[32,2048]{1,0:T(8,128)(2,1)S(1)} %fusion.28), channel_id=1, source_target_pairs={{8,0},{16,8},{24,16},{32,24},{40,32},{48,40},{56,48},{64,56},{72,6... | collective-permute-start | bytes 393224 | tf_op jit(solution)/shard_map/ppermute | solution.py:19
  86.3 217.7 %all-reduce.6.cloned.1.call-start = ((), (), s32[]{:S(2)}) async-start(), calls=%async_computation.3 | async-start | bytes 524288 | tf_op jit(solution)/shard_map/psum | solution.py:56
  367.1 15.8 %all-to-all-start.1 = ((f32[8,32,256]{2,1,0:T(8,128)}), f32[8,32,256]{2,1,0:T(8,128)S(1)}, u32[]{:S(2)}, u32[]{:S(2)}) async-start(f32[8,32,256]{2,1,0:T(8,128)} %bitcast.26), calls=%async_computation.1 | async-start | bytes 524288 | tf_op jit(solution)/shard_map/all_to_all | solution.py:59
Sparse Core Ops, SparseCore 0:
  86.4 64.3 all-reduce.3
  154.0 149.9 all-reduce.5
